TPU v7x, 32 devices: a whole 2x2x4 slice. The times are simulated.
32 devices in a mesh: dp: 4 (over y, x), fsdp: 2 (over core), ctx: 4 (over z).
Axes of the slice: x: 2, y: 2, z: 4, core: 2. Of those that a mesh axis runs over, the one named last changes fastest.
Arguments:
- tokens: bfloat16 [16384, 8192], P(('dp', 'ctx')), may hold values from -6 to 6
- grad_hidden: bfloat16 [16384, 256], P(('dp', 'ctx'), 'fsdp'), may hold values from -0.0625 to 0.0625
- master: float32 [256, 8192], P(('fsdp', 'ctx')), may hold values from -3 to 3
- first_moment: float32 [256, 8192], P(('fsdp', 'ctx')), may hold values from -2 to 2
- second_moment: float32 [256, 8192], P(('fsdp', 'ctx')), may hold values from 0.01 to 1
- clip_scale: float32 [], replicated, may hold values from 0.2 to 1
Outputs:
- new_weights: bfloat16 [256, 8192], P('fsdp')
- new_master: float32 [256, 8192], P(('fsdp', 'ctx'))
- new_first: float32 [256, 8192], P(('fsdp', 'ctx'))
- new_second: float32 [256, 8192], P(('fsdp', 'ctx'))
All inputs are finite; a program needn't handle non-finite values.
Results may differ from a plain program's by a relative error of at most 0.005.
Values may be sent and summed in bfloat16 or wider, within the bound.
A program may use at most 128 MiB of HBM per device.

v0:
```python
import jax
import jax.numpy as jnp
from jax import lax
from jax.sharding import PartitionSpec as P

STEP = 10
BETA_ONE = 0.9
BETA_TWO = 0.95
EPSILON = 1e-08
LEARNING_RATE = 0.02
DECAY = 0.1


def contract(columns, tokens):
    return lax.dot_general(
        columns, tokens, (((0,), (0,)), ((), ())), preferred_element_type=jnp.float32
    )


def adamw(grad_sum, master, first_moment, second_moment, clip_scale):
    scaled = clip_scale * grad_sum
    first_new = BETA_ONE * first_moment + (1.0 - BETA_ONE) * scaled
    second_new = BETA_TWO * second_moment + (1.0 - BETA_TWO) * scaled * scaled
    first_hat = first_new / (1.0 - BETA_ONE**STEP)
    second_hat = second_new / (1.0 - BETA_TWO**STEP)
    update = first_hat / (jnp.sqrt(second_hat) + EPSILON)
    fresh_master = master - LEARNING_RATE * (update + DECAY * master)
    return (fresh_master, first_new, second_new)


def per_device(tokens, grad_hidden, master, first_moment, second_moment, clip_scale):
    ctx_count = lax.axis_size("ctx")
    dp_count = lax.axis_size("dp")
    row_dev = master.shape[0]
    width = tokens.shape[1]
    piece_rows = row_dev // dp_count
    tok_rows = grad_hidden.shape[0]
    reordered = (
        grad_hidden.reshape(tok_rows, ctx_count, dp_count, piece_rows)
        .transpose(0, 2, 1, 3)
        .reshape(tok_rows, ctx_count * dp_count * piece_rows)
    )
    partial_terms = contract(reordered, tokens).astype(jnp.bfloat16)
    piece_terms = partial_terms.reshape(dp_count * ctx_count, piece_rows, width)
    received = lax.all_to_all(piece_terms, ("dp", "ctx"), split_axis=0, concat_axis=0, tiled=True)
    piece_grad = jnp.sum(received, axis=0, dtype=jnp.float32)
    offset = lax.axis_index("dp") * piece_rows
    master_piece = lax.dynamic_slice_in_dim(master, offset, piece_rows, 0)
    first_piece = lax.dynamic_slice_in_dim(first_moment, offset, piece_rows, 0)
    second_piece = lax.dynamic_slice_in_dim(second_moment, offset, piece_rows, 0)
    fresh_piece, first_fresh, second_fresh = adamw(
        piece_grad, master_piece, first_piece, second_piece, clip_scale
    )
    new_master, new_first, new_second = (
        lax.all_gather(fresh_piece.astype(jnp.bfloat16), "dp", axis=0, tiled=True).astype(
            fresh_piece.dtype
        ),
        lax.all_gather(first_fresh.astype(jnp.bfloat16), "dp", axis=0, tiled=True).astype(
            first_fresh.dtype
        ),
        lax.all_gather(second_fresh.astype(jnp.bfloat16), "dp", axis=0, tiled=True).astype(
            second_fresh.dtype
        ),
    )
    new_weights = lax.all_gather(new_master.astype(jnp.bfloat16), "ctx", axis=0, tiled=True)
    return (new_weights, new_master, new_first, new_second)


def solution(mesh):
    in_specs = (
        P(("dp", "ctx"), None),
        P(("dp", "ctx"), "fsdp"),
        P(("fsdp", "ctx"), None),
        P(("fsdp", "ctx"), None),
        P(("fsdp", "ctx"), None),
        P(),
    )
    out_specs = (
        P("fsdp", None),
        P(("fsdp", "ctx"), None),
        P(("fsdp", "ctx"), None),
        P(("fsdp", "ctx"), None),
    )
    return jax.shard_map(
        per_device, mesh=mesh, in_specs=in_specs, out_specs=out_specs, check_vma=False
    )
```

profile of v0, /device:TPU:0, one launch (start us, length us, event | category | flops | bytes accessed | tf_op | source)
XLA Modules:
  0.0 141.5 jit_solution(3113973933799284460)
XLA Ops:
  7.2 1.1 copy.10
  8.3 9.5 %fusion = bf16[16,8,8192]{2,1,0:T(8,128)(2,1)} fusion(bf16[1024,128]{0,1:T(8,128)(2,1)S(1)} %bitcast.8, bf16[1024,8192]{1,0:T(8,128)(2,1)} %param.6), kind=kOutput, calls=%fused_computation.1 | convolution fusion | flops 2148532224 | bytes 19136512 | tf_op jit(solution)/shard_map/dot_general | solution.py:15
  17.7 8.3 %all-to-all-start = ((bf16[16,8,8192]{2,1,0:T(8,128)(2,1)}), bf16[16,8,8192]{2,1,0:T(8,128)(2,1)S(1)}, u32[]{:S(2)}, u32[]{:S(2)}) async-start(bf16[16,8,8192]{2,1,0:T(8,128)(2,1)} %fusion), calls=%async_computation | async-start | bytes 4194304 | tf_op jit(solution)/shard_map/all_to_all | solution.py:45
  26.1 0.0 all-gather.2.cloned.1.call-start
  26.8 49.2 %all-to-all-done = bf16[16,8,8192]{2,1,0:T(8,128)(2,1)S(1)} async-done(((bf16[16,8,8192]{2,1,0:T(8,128)(2,1)}), bf16[16,8,8192]{2,1,0:T(8,128)(2,1)S(1)}, u32[]{:S(2)}, u32[]{:S(2)}) %all-to-all-start) | async-done | bytes 2097184 | tf_op jit(solution)/shard_map/all_to_all | solution.py:45
  76.0 0.3 convert_reduce_fusion
  76.3 1.4 fusion.3
  77.7 9.8 %all_gather.12 = bf16[32,8192]{1,0:T(8,128)(2,1)} all-gather(bf16[8,8192]{1,0:T(8,128)(2,1)S(1)} %get-tuple-element.5), channel_id=1, replica_groups=mesh['dp'=4,'fsdp'=2,'ctx'=4] {'dp'}, dimensions={0}, use_global_device_ids=true | all-gather | bytes 655360 | tf_op jit(solution)/shard_map/all_gather | solution.py:55
  87.4 0.0 all-gather.2.cloned.1.call-update
  87.5 2.1 %convert_element_type.28 = f32[32,8192]{1,0:T(8,128)} convert(bf16[32,8192]{1,0:T(8,128)(2,1)} %all_gather.12) | non-fusion elementwise | flops 262144 | bytes 1572864 | tf_op jit(solution)/shard_map/convert_element_type | solution.py:55
  89.5 10.0 %all_gather.15 = bf16[32,8192]{1,0:T(8,128)(2,1)S(1)} all-gather(bf16[8,8192]{1,0:T(8,128)(2,1)S(1)} %get-tuple-element.4), channel_id=1, replica_groups=mesh['dp'=4,'fsdp'=2,'ctx'=4] {'dp'}, dimensions={0}, use_global_device_ids=true | all-gather | bytes 655360 | tf_op jit(solution)/shard_map/all_gather | solution.py:61
  99.5 1.0 convert_element_type.32
  100.6 9.3 %all_gather.14 = bf16[32,8192]{1,0:T(8,128)(2,1)S(1)} all-gather(bf16[8,8192]{1,0:T(8,128)(2,1)S(1)} %get-tuple-element.6), channel_id=1, replica_groups=mesh['dp'=4,'fsdp'=2,'ctx'=4] {'dp'}, dimensions={0}, use_global_device_ids=true | all-gather | bytes 655360 | tf_op jit(solution)/shard_map/all_gather | solution.py:58
  109.9 1.0 convert_element_type.30
  111.0 20.6 %all-gather.2.cloned.1.call-done = bf16[128,8192]{1,0:T(8,128)(2,1)} async-done(((bf16[32,8192]{1,0:T(8,128)(2,1)}), bf16[128,8192]{1,0:T(8,128)(2,1)}) %all-gather.2.cloned.1.call-update) | async-done | bytes 2097168 | tf_op jit(solution)/shard_map/all_gather | solution.py:65
  131.6 3.1 %copy.14 = bf16[128,8192]{1,0:T(8,128)(2,1)} copy(bf16[128,8192]{1,0:T(8,128)(2,1)} %all-gather.2.cloned.1.call-done) | data formatting | bytes 4194304
  (1 shorter events, 0.0 us)
Async XLA Ops:
  17.7 58.3 %all-to-all-start = ((bf16[16,8,8192]{2,1,0:T(8,128)(2,1)}), bf16[16,8,8192]{2,1,0:T(8,128)(2,1)S(1)}, u32[]{:S(2)}, u32[]{:S(2)}) async-start(bf16[16,8,8192]{2,1,0:T(8,128)(2,1)} %fusion), calls=%async_computation | async-start | bytes 4194304 | tf_op jit(solution)/shard_map/all_to_all | solution.py:45
  26.1 105.5 %all-gather.2.cloned.1.call-start = ((), (), s32[]{:S(2)}) async-start(), calls=%async_computation.1 | async-start | bytes 2621440 | tf_op jit(solution)/shard_map/all_gather | solution.py:65
Sparse Core Ops, SparseCore 0:
  87.6 43.9 all-gather.1
where the time goes:
time: 142 us
  waiting for transfers between devices  69.9 us (49%)
  blocking collectives  29.1 us (20%)
  between operations  14.7 us (10%)
  matrix products  9.45 us (7%)
  starting transfers between devices  8.35 us (6%)
  other arithmetic  5.81 us (4%)
  local copies, waits for them, and re-layouts  4.2 us (3%)
    all_to_all x1, waiting for transfers between devices, per_device(): lax.all_to_all(piece_terms, ('dp', 'ctx'), split_axis=0, concat_axis=0, t...  49.2 us
    all_gather x1, waiting for transfers between devices, per_device(): lax.all_gather(new_master.astype(jnp.bfloat16), 'ctx', axis=0, tiled=True)  20.6 us
    all_gather x1, blocking collectives, per_device(): lax.all_gather(second_fresh.astype(jnp.bfloat16), 'dp', axis=0, tiled=True)  10 us
    all_gather x1, blocking collectives, per_device(): lax.all_gather(fresh_piece.astype(jnp.bfloat16), 'dp', axis=0, tiled=True)  9.78 us
    dot_general x1, matrix products, contract(): lax.dot_general(columns, tokens, (((0,), (0,)), ((), ())), preferred_elem...  9.45 us
    all_gather x1, blocking collectives, per_device(): lax.all_gather(first_fresh.astype(jnp.bfloat16), 'dp', axis=0, tiled=True)  9.32 us
    all_to_all x1, starting transfers between devices, per_device(): lax.all_to_all(piece_terms, ('dp', 'ctx'), split_axis=0, concat_axis=0, t...  8.31 us
    unnamed x2, local copies, waits for them, and re-layouts  4.18 us
  transfers between devices with their start and end apart: 2, of which 2 were waited for; matrix products, arithmetic and copies ran while one was open for 3% of the time, Pallas kernels for 0%

commit v1 on v0

--- a/solution.py
+++ b/solution.py
@@ -9,6 +9,18 @@
 EPSILON = 1e-08
 LEARNING_RATE = 0.02
 DECAY = 0.1
+
+
+def collect(value, axis, dim):
+    ways, here = (lax.axis_size(axis), lax.axis_index(axis))
+    grown, reach = (value, 1)
+    while reach < ways:
+        theirs = lax.ppermute(grown, axis, [(d, d ^ reach) for d in range(ways)])
+        mine_first = jnp.concatenate([grown, theirs], axis=dim)
+        theirs_first = jnp.concatenate([theirs, grown], axis=dim)
+        grown = jnp.where(here & reach == 0, mine_first, theirs_first)
+        reach = 2 * reach
+    return grown
 
 
 def contract(columns, tokens):
@@ -55,9 +67,7 @@
         lax.all_gather(fresh_piece.astype(jnp.bfloat16), "dp", axis=0, tiled=True).astype(
             fresh_piece.dtype
         ),
-        lax.all_gather(first_fresh.astype(jnp.bfloat16), "dp", axis=0, tiled=True).astype(
-            first_fresh.dtype
-        ),
+        collect(first_fresh.astype(jnp.bfloat16), "dp", 0).astype(first_fresh.dtype),
         lax.all_gather(second_fresh.astype(jnp.bfloat16), "dp", axis=0, tiled=True).astype(
             second_fresh.dtype
         ),

time: 142 us -> 142 us (level)
  blocking collectives: 29.1 us -> 19.1 us
  waiting for transfers between devices: 69.9 us -> 76.3 us
  starting transfers between devices: 8.35 us -> 11.8 us
    all_gather x1 -> x0, blocking collectives: 9.32 us -> none  [per_device(): lax.all_gather(first_fresh.astype(jnp.bfloat16), 'dp', axis=0, tiled=True)]
    ppermute x0 -> x2, starting transfers between devices: none -> 3.47 us  [collect(): theirs = lax.ppermute(grown, axis, [(d, d ^ reach) for d in range(ways)])]
    ppermute x0 -> x2, waiting for transfers between devices: none -> 3.3 us  [collect(): theirs = lax.ppermute(grown, axis, [(d, d ^ reach) for d in range(ways)])]
    all_gather x1, waiting for transfers between devices: 20.6 us -> 23.8 us  [per_device(): lax.all_gather(new_master.astype(jnp.bfloat16), 'ctx', axis=0, tiled=True)]
  transfers between devices with their start and end apart: 2 -> 4, of which waited for: 2 -> 3; matrix products, arithmetic and copies ran while one was open for 3% -> 3% of each run, Pallas kernels for 0% -> 0%
where the time goes in v1:
time: 142 us
  waiting for transfers between devices  76.3 us (54%)
  blocking collectives  19.1 us (13%)
  between operations  14.7 us (10%)
  starting transfers between devices  11.8 us (8%)
  matrix products  9.45 us (7%)
  other arithmetic  5.86 us (4%)
  local copies, waits for them, and re-layouts  4.2 us (3%)
    all_to_all x1, waiting for transfers between devices, per_device(): lax.all_to_all(piece_terms, ('dp', 'ctx'), split_axis=0, concat_axis=0, t...  49.2 us
    all_gather x1, waiting for transfers between devices, per_device(): lax.all_gather(new_master.astype(jnp.bfloat16), 'ctx', axis=0, tiled=True)  23.8 us
    all_gather x1, blocking collectives, per_device(): lax.all_gather(fresh_piece.astype(jnp.bfloat16), 'dp', axis=0, tiled=True)  9.79 us
    dot_general x1, matrix products, contract(): lax.dot_general(columns, tokens, (((0,), (0,)), ((), ())), preferred_elem...  9.45 us
    all_gather x1, blocking collectives, per_device(): lax.all_gather(second_fresh.astype(jnp.bfloat16), 'dp', axis=0, tiled=True)  9.35 us
    all_to_all x1, starting transfers between devices, per_device(): lax.all_to_all(piece_terms, ('dp', 'ctx'), split_axis=0, concat_axis=0, t...  8.31 us
    unnamed x2, local copies, waits for them, and re-layouts  4.18 us
    ppermute x2, starting transfers between devices, collect(): theirs = lax.ppermute(grown, axis, [(d, d ^ reach) for d in range(ways)])  3.47 us
  transfers between devices with their start and end apart: 4, of which 3 were waited for; matrix products, arithmetic and copies ran while one was open for 3% of the time, Pallas kernels for 0%

profile of v1, /device:TPU:0, one launch (start us, length us, event | category | flops | bytes accessed | tf_op | source)
XLA Modules:
  0.0 141.5 jit_solution(5367716661081964570)
XLA Ops:
  7.2 1.1 copy.10
  8.3 9.5 %fusion = bf16[16,8,8192]{2,1,0:T(8,128)(2,1)} fusion(bf16[1024,128]{0,1:T(8,128)(2,1)S(1)} %bitcast.8, bf16[1024,8192]{1,0:T(8,128)(2,1)} %param.6), kind=kOutput, calls=%fused_computation.1 | convolution fusion | flops 2148532224 | bytes 19136512 | tf_op jit(solution)/shard_map/dot_general | solution.py:27
  17.7 8.3 %all-to-all-start = ((bf16[16,8,8192]{2,1,0:T(8,128)(2,1)}), bf16[16,8,8192]{2,1,0:T(8,128)(2,1)S(1)}, u32[]{:S(2)}, u32[]{:S(2)}) async-start(bf16[16,8,8192]{2,1,0:T(8,128)(2,1)} %fusion), calls=%async_computation | async-start | bytes 4194304 | tf_op jit(solution)/shard_map/all_to_all | solution.py:57
  26.1 0.0 all-gather.2.cloned.1.call-start
  26.8 49.2 %all-to-all-done = bf16[16,8,8192]{2,1,0:T(8,128)(2,1)S(1)} async-done(((bf16[16,8,8192]{2,1,0:T(8,128)(2,1)}), bf16[16,8,8192]{2,1,0:T(8,128)(2,1)S(1)}, u32[]{:S(2)}, u32[]{:S(2)}) %all-to-all-start) | async-done | bytes 2097184 | tf_op jit(solution)/shard_map/all_to_all | solution.py:57
  76.0 0.3 convert_reduce_fusion
  76.3 1.4 fusion.4
  77.7 9.8 %all_gather.9 = bf16[32,8192]{1,0:T(8,128)(2,1)} all-gather(bf16[8,8192]{1,0:T(8,128)(2,1)S(1)} %get-tuple-element.5), channel_id=1, replica_groups=mesh['dp'=4,'fsdp'=2,'ctx'=4] {'dp'}, dimensions={0}, use_global_device_ids=true | all-gather | bytes 655360 | tf_op jit(solution)/shard_map/all_gather | solution.py:67
  87.4 0.0 all-gather.2.cloned.1.call-update
  87.5 1.7 %collective-permute-start = (bf16[8,8192]{1,0:T(8,128)(2,1)S(1)}, bf16[8,8192]{1,0:T(8,128)(2,1)S(1)}, u32[]{:S(2)}, u32[]{:S(2)}) collective-permute-start(bf16[8,8192]{1,0:T(8,128)(2,1)S(1)} %get-tuple-element.6), channel_id=1, source_target_pairs={{0,8},{8,0},{16,24},{24,16},{1,9},{9,1},{17,25},{25,17},{2,10},{10... | collective-permute-start | bytes 393224 | tf_op jit(solution)/shard_map/ppermute | solution.py:18
  89.2 3.3 %collective-permute-done = bf16[8,8192]{1,0:T(8,128)(2,1)S(1)} collective-permute-done((bf16[8,8192]{1,0:T(8,128)(2,1)S(1)}, bf16[8,8192]{1,0:T(8,128)(2,1)S(1)}, u32[]{:S(2)}, u32[]{:S(2)}) %collective-permute-start) | collective-permute-done | bytes 131104 | tf_op jit(solution)/shard_map/ppermute | solution.py:18
  92.6 1.7 %collective-permute-start.1 = (bf16[16,8192]{1,0:T(8,128)(2,1)S(1)}, bf16[16,8192]{1,0:T(8,128)(2,1)S(1)}, u32[]{:S(2)}, u32[]{:S(2)}) collective-permute-start(bf16[16,8192]{1,0:T(8,128)(2,1)S(1)} %maximum_select_fusion.1), channel_id=1, source_target_pairs={{0,16},{8,24},{16,0},{24,8},{1,17},{9,25},{17,1},{25,9},{2,18},{10... | collective-permute-start | bytes 786440 | tf_op jit(solution)/shard_map/ppermute | solution.py:18
  94.3 2.1 %convert_element_type.28 = f32[32,8192]{1,0:T(8,128)} convert(bf16[32,8192]{1,0:T(8,128)(2,1)} %all_gather.9) | non-fusion elementwise | flops 262144 | bytes 1572864 | tf_op jit(solution)/shard_map/convert_element_type | solution.py:67
  96.4 9.3 %all_gather.11 = bf16[32,8192]{1,0:T(8,128)(2,1)S(1)} all-gather(bf16[8,8192]{1,0:T(8,128)(2,1)S(1)} %get-tuple-element.4), channel_id=1, replica_groups=mesh['dp'=4,'fsdp'=2,'ctx'=4] {'dp'}, dimensions={0}, use_global_device_ids=true | all-gather | bytes 655360 | tf_op jit(solution)/shard_map/all_gather | solution.py:71
  105.7 1.0 convert_element_type.32
  106.8 0.0 collective-permute-done.1
  106.8 1.0 fusion.1
  107.8 23.8 %all-gather.2.cloned.1.call-done = bf16[128,8192]{1,0:T(8,128)(2,1)} async-done(((bf16[32,8192]{1,0:T(8,128)(2,1)}), bf16[128,8192]{1,0:T(8,128)(2,1)}) %all-gather.2.cloned.1.call-update) | async-done | bytes 2097168 | tf_op jit(solution)/shard_map/all_gather | solution.py:75
  131.6 3.1 %copy.14 = bf16[128,8192]{1,0:T(8,128)(2,1)} copy(bf16[128,8192]{1,0:T(8,128)(2,1)} %all-gather.2.cloned.1.call-done) | data formatting | bytes 4194304
  (2 shorter events, 0.1 us)
Async XLA Ops:
  17.7 58.3 %all-to-all-start = ((bf16[16,8,8192]{2,1,0:T(8,128)(2,1)}), bf16[16,8,8192]{2,1,0:T(8,128)(2,1)S(1)}, u32[]{:S(2)}, u32[]{:S(2)}) async-start(bf16[16,8,8192]{2,1,0:T(8,128)(2,1)} %fusion), calls=%async_computation | async-start | bytes 4194304 | tf_op jit(solution)/shard_map/all_to_all | solution.py:57
  26.1 105.5 %all-gather.2.cloned.1.call-start = ((), (), s32[]{:S(2)}) async-start(), calls=%async_computation.1 | async-start | bytes 2621440 | tf_op jit(solution)/shard_map/all_gather | solution.py:75
  87.5 5.0 %collective-permute-start = (bf16[8,8192]{1,0:T(8,128)(2,1)S(1)}, bf16[8,8192]{1,0:T(8,128)(2,1)S(1)}, u32[]{:S(2)}, u32[]{:S(2)}) collective-permute-start(bf16[8,8192]{1,0:T(8,128)(2,1)S(1)} %get-tuple-element.6), channel_id=1, source_target_pairs={{0,8},{8,0},{16,24},{24,16},{1,9},{9,1},{17,25},{25,17},{2,10},{10... | collective-permute-start | bytes 393224 | tf_op jit(solution)/shard_map/ppermute | solution.py:18
  92.6 14.2 %collective-permute-start.1 = (bf16[16,8192]{1,0:T(8,128)(2,1)S(1)}, bf16[16,8192]{1,0:T(8,128)(2,1)S(1)}, u32[]{:S(2)}, u32[]{:S(2)}) collective-permute-start(bf16[16,8192]{1,0:T(8,128)(2,1)S(1)} %maximum_select_fusion.1), channel_id=1, source_target_pairs={{0,16},{8,24},{16,0},{24,8},{1,17},{9,25},{17,1},{25,9},{2,18},{10... | collective-permute-start | bytes 786440 | tf_op jit(solution)/shard_map/ppermute | solution.py:18
Sparse Core Ops, SparseCore 0:
  87.6 43.9 all-gather.1
